TPU v7x, 128 devices: a whole 4x4x4 slice. The times are simulated.
128 devices in a mesh: band: 32 (over z, x, core), lev: 4 (over y).
Axes of the slice: x: 4, y: 4, z: 4, core: 2. Of those that a mesh axis runs over, the one named last changes fastest.
Arguments:
- air_fourier_coefficients: float32 [4, 16, 1280, 256], P('lev', None, 'band'), may hold values from -6 to 6
- quadrature_factor: float32 [1280], P('band'), may hold values from 0.5 to 1.5
- associated_polynomial_table: bfloat16 [128, 1280, 1280], P('band'), may hold values from -6 to 6
- east_west_harmonic: int32 [128], replicated, may hold values from 0 to 1279, as said below
- boundary_diffusion: float32 [4, 16, 16, 1280], P('lev', None, None, 'band'), may hold values from -0.25 to 0.25
- bulk_transfer_coefficient: float32 [4, 1280], P('lev', 'band'), may hold values from 0.1 to 1
- skin_heat_earlier: float32 [12, 4, 1280, 256], P(None, 'lev', 'band'), may hold values from -6 to 6
- sea_boundary_values: float32 [4, 1024, 1440], P('lev', 'band'), may hold values from -6 to 6
- sea_damping_speed: float32 [4, 1024, 1440], P('lev', 'band'), may hold values from 0.02 to 2
- sea_coupling_matrix: float32 [4, 4], replicated, may hold values from -1.75 to 1.75
- patch_active_entries: int32 [32], P('band'), may hold values from 8 to 32, as said below
- sea_southern_parallel: int32 [1024], P('band'), may hold values from 0 to 1278, as said below
- sea_northern_share: float32 [1024], P('band'), may hold values from 0 to 1
- air_paired_cells: int32 [2, 1280], P(None, 'band'), may hold values from 0 to 1023, as said below
- air_second_share: float32 [1280], P('band'), may hold values from 0 to 1
Outputs:
- air_coefficients_end: float32 [4, 16, 1280, 256], P('lev', None, 'band')
- sea_values_end: float32 [4, 1024, 1440], P('lev', 'band')
- skin_heat_newest: float32 [12, 4, 1280, 256], P(None, 'lev', 'band')
Inputs may be any that keep to these rules, and one draw needn't show every extreme that they name: `east_west_harmonic`: Distinct; positions 2 j and 2 j + 1 hold m and 1279 - m for some m below 640; 0 is among them. `patch_active_entries`: the live slots of a tile come first; the last tile is full. For a slot of tile t, sea_southern_parallel and sea_southern_parallel + 1 lie in t * 40 - 8 to (t + 1) * 40 + 7; they do not decrease along a tile's live slots. `air_paired_cells`: for a latitude of band t both taps are live slots of tiles t - 1, t or t + 1, the first one of tile t, and the two differ.
All inputs are finite; a program needn't handle non-finite values.
Results may differ from a plain program's by a relative error of at most 0.014.
Values may be sent and summed in bfloat16 or wider, within the bound.
No kernel may reach another device: no remote copies, remote signals or barrier semaphores. Data moves between devices by JAX's collectives and lax.ppermute only.
A program may use at most 64 MiB of HBM per device.

v0:
```python
import math
import jax
import jax.numpy as jnp
from jax import lax
from jax.sharding import PartitionSpec as P

PARALLEL_NUMBER = 1280
MARG = 8
degree_damping = 2e-06
ocean_step = 0.5
mixing_diagonal = 0.95
synth_divisor = 4.0


def with_halo(shard, sides, width):
    for axis, dim in sides:
        size, length = (lax.axis_size(axis), shard.shape[dim])
        up = [(i, (i + 1) % size) for i in range(size - 1)]
        down = [(j, i) for i, j in up]
        last = lax.slice_in_dim(shard, length - width, length, axis=dim)
        first = lax.slice_in_dim(shard, 0, width, axis=dim)
        before = lax.ppermute(last, axis, up)
        after = lax.ppermute(first, axis, down)
        shard = jnp.concatenate([before, shard, after], axis=dim)
    return shard


def damping_table(wave_values, degree_count):
    degrees = wave_values[:, None] + jnp.arange(degree_count, dtype=jnp.int32)[None, :]
    degree_float = degrees.astype(jnp.float32)
    factor = 1.0 / (1.0 + degree_damping * degree_float * (degree_float + 1.0))
    return jnp.where(degrees < degree_count, factor, jnp.zeros_like(factor))


def zonal_table(wave_values, lon_count):
    longitude = jnp.arange(lon_count, dtype=jnp.int32)
    phases = wave_values[:, None] * longitude[None, :] % lon_count
    angles = phases.astype(jnp.float32) * (2.0 * math.pi / lon_count)
    stacked = jnp.stack([jnp.cos(angles), -jnp.sin(angles)], axis=1)
    return stacked.reshape(2 * wave_values.shape[0], lon_count).astype(jnp.bfloat16)


def padded_transform(values, tables, damping):
    row_count = values.shape[0]
    lat_count = values.shape[1]
    wave_count = tables.shape[0]
    shaped = values.reshape(row_count, lat_count, wave_count, 2)
    spectral = jnp.einsum("rlmc,mln->rmnc", shaped, tables, preferred_element_type=jnp.float32)
    damped = (spectral * damping[None, :, :, None]).astype(jnp.bfloat16)
    synthesis = jnp.einsum("rmnc,mln->rlmc", damped, tables, preferred_element_type=jnp.float32)
    synthesis = synthesis * (1.0 / (synth_divisor * math.sqrt(tables.shape[2])))
    return synthesis.astype(jnp.bfloat16).reshape(row_count, lat_count, wave_count * 2)


def per_device(
    air_fourier_coefficients,
    quadrature_factor,
    associated_polynomial_table,
    east_west_harmonic,
    boundary_diffusion,
    bulk_transfer_coefficient,
    skin_heat_earlier,
    sea_boundary_values,
    sea_damping_speed,
    sea_coupling_matrix,
    patch_active_entries,
    sea_southern_parallel,
    sea_northern_share,
    air_paired_cells,
    air_second_share,
):
    band_index = lax.axis_index("band")
    lev_index = lax.axis_index("lev")
    field_local = air_fourier_coefficients.shape[0]
    height_pile = air_fourier_coefficients.shape[1]
    lat_local = air_fourier_coefficients.shape[2]
    column_count = air_fourier_coefficients.shape[3]
    row_count = field_local * height_pile
    owned = associated_polynomial_table.shape[0]
    degree_count = associated_polynomial_table.shape[2]
    wave_values = lax.dynamic_slice_in_dim(east_west_harmonic, band_index * owned, owned, 0)
    damping = damping_table(wave_values, degree_count)

    def transform(values):
        return padded_transform(values, associated_polynomial_table, damping)

    identity_block = jnp.eye(height_pile, dtype=jnp.float32)[None, :, :, None]
    mixing = (
        mixing_diagonal * identity_block
        + boundary_diffusion
        - jnp.transpose(boundary_diffusion, (0, 2, 1, 3))
    )
    weight = quadrature_factor * (1.0 / math.sqrt(PARALLEL_NUMBER))

    def march_air_model(air_model_present, skin_heat_present):
        scaled = (air_model_present * weight[None, None, :, None]).astype(jnp.bfloat16)
        scaled = scaled.reshape(row_count, lat_local, column_count)
        by_wave = lax.all_to_all(scaled, "band", split_axis=2, concat_axis=1, tiled=True)
        synthesis = transform(by_wave)
        returned = lax.all_to_all(synthesis, "band", split_axis=1, concat_axis=2, tiled=True)
        synthesis_field = returned.reshape(
            field_local, height_pile, lat_local, column_count
        ).astype(jnp.float32)
        halfway_point = air_model_present - synthesis_field
        bottom_sheet = bulk_transfer_coefficient[:, :, None] * (
            skin_heat_present - halfway_point[:, height_pile - 1]
        )
        mixed_state = jnp.einsum(
            "flpa,fpac->flac", mixing, halfway_point, precision=lax.Precision.HIGHEST
        )
        mixed_state = mixed_state.at[:, height_pile - 1].add(bottom_sheet)
        return (mixed_state, bottom_sheet.astype(jnp.bfloat16))

    air_coefficients_end, forcing_series = lax.scan(
        march_air_model, air_fourier_coefficients, skin_heat_earlier
    )
    slot_rows = sea_boundary_values.shape[1]
    extended = with_halo(forcing_series, (("band", 2),), MARG)
    rim_rows = lat_local + 2 * MARG
    lowest = band_index * lat_local - MARG
    live_slot = jnp.arange(slot_rows, dtype=jnp.int32) < patch_active_entries[0]
    offsets = (sea_southern_parallel - lowest)[:, None]
    rim_index = jnp.arange(rim_rows, dtype=jnp.int32)[None, :]
    low_weight = jnp.where(live_slot, 1.0 - sea_northern_share, jnp.zeros_like(sea_northern_share))[
        :, None
    ]
    high_weight = jnp.where(live_slot, sea_northern_share, jnp.zeros_like(sea_northern_share))[
        :, None
    ]
    flux_taps = jnp.where(rim_index == offsets, low_weight, 0.0) + jnp.where(
        rim_index == offsets + 1, high_weight, 0.0
    )
    flux_taps = flux_taps.astype(jnp.bfloat16)
    ocean_flux = jnp.einsum(
        "sa,kfac->kfsc", flux_taps, extended, preferred_element_type=jnp.float32
    ).astype(jnp.bfloat16)
    lon_count = sea_boundary_values.shape[2]
    zonal_basis = zonal_table(east_west_harmonic, lon_count)
    synth_scale = 1.0 / math.sqrt(zonal_basis.shape[0])
    skew_full = sea_coupling_matrix - sea_coupling_matrix.T
    skew_mine = lax.dynamic_slice_in_dim(skew_full, lev_index * field_local, field_local, 0)

    def ocean_advance(ocean_now, flux_now):
        forcing = (
            jnp.einsum("fsc,cx->fsx", flux_now, zonal_basis, preferred_element_type=jnp.float32)
            * synth_scale
        )
        gathered = lax.all_gather(ocean_now.astype(jnp.bfloat16), "lev", axis=0, tiled=True)
        coupled = jnp.zeros_like(ocean_now)
        for field_index in range(gathered.shape[0]):
            coupled = (
                coupled
                + skew_mine[:, field_index][:, None, None]
                * gathered[field_index].astype(jnp.float32)[None]
            )
        updated = (ocean_now + ocean_step * (coupled - forcing)) / (
            1.0 + ocean_step * sea_damping_speed
        )
        return (updated, updated.astype(jnp.bfloat16))

    sea_values_end, ocean_wave = lax.scan(ocean_advance, sea_boundary_values, ocean_flux)
    ocean_coef = jnp.einsum(
        "kfsx,cx->kfsc", ocean_wave, zonal_basis, preferred_element_type=jnp.float32
    )
    ocean_coef = (ocean_coef * (1.0 / math.sqrt(lon_count))).astype(jnp.bfloat16)
    neighbours = with_halo(ocean_coef, (("band", 2),), slot_rows)
    base_slot = (band_index - 1) * slot_rows
    slot_index = jnp.arange(3 * slot_rows, dtype=jnp.int32)[None, :]
    first_local = (air_paired_cells[0] - base_slot)[:, None]
    second_local = (air_paired_cells[1] - base_slot)[:, None]
    return_taps = jnp.where(
        slot_index == first_local, (1.0 - air_second_share)[:, None], 0.0
    ) + jnp.where(slot_index == second_local, air_second_share[:, None], 0.0)
    return_taps = return_taps.astype(jnp.bfloat16)
    skin_heat_newest = jnp.einsum(
        "ga,kfac->kfgc", return_taps, neighbours, preferred_element_type=jnp.float32
    )
    return (air_coefficients_end, sea_values_end, skin_heat_newest)


def solution(mesh):
    return jax.shard_map(
        per_device,
        mesh=mesh,
        in_specs=(
            P("lev", None, "band", None),
            P("band"),
            P("band", None, None),
            P(),
            P("lev", None, None, "band"),
            P("lev", "band"),
            P(None, "lev", "band", None),
            P("lev", "band", None),
            P("lev", "band", None),
            P(),
            P("band"),
            P("band"),
            P("band"),
            P(None, "band"),
            P("band"),
        ),
        out_specs=(
            P("lev", None, "band", None),
            P("lev", "band", None),
            P(None, "lev", "band", None),
        ),
        check_vma=False,
    )
```

profile of v0, /device:TPU:15, one launch (start us, length us, event | category | flops | bytes accessed | tf_op | source)
XLA Modules:
  0.0 1154.0 jit_solution(6040955849517082085)
XLA Ops:
  4.1 916.9 %while.29 = (s32[]{:T(128)}, f32[1,16,40,256]{3,1,2,0:T(8,128)S(1)}, bf16[12,1,40,256]{3,2,1,0:T(8,128)(2,1)S(1)}, f32[40]{0:T(128)S(1)}, bf16[4,1280,1280]{2,1,...) while((s32[]{:T(128)}, ...), condition=%wide.region_1.2_spmd.clone, body=%wide.region_0.1_spmd.clone.sunk | while | flops 871552000 | bytes 31130164 | solution.py:114
  7.8 8.7 all-to-all-start
  16.6 8.1 all-to-all-done
  28.9 15.2 %fusion.110 = bf16[4,16,2,1280]{3,1,2,0:T(8,128)(2,1)} fusion(bf16[4,1280,1280]{2,1,0:T(8,128)(2,1)} %get-tuple-element.499, bf16[16,1280,4,2]{1,0,3,2:T(8,128)(2,1)S(1)} %reshape.391, f32[4,1280]{1,0:T(4,128)S(1)} %divide_select_fusion.2), kind=kOutput, calls=%fused_computation.17.clone.1 | convolution fusion | flops 839516160 | bytes 13783040 | tf_op jit(solution)/shard_map/while/body/eval_jaxpr/rmnc,mln->rlmc/dot_general | solution.py:50
  58.0 6.2 all-to-all-done.1
  92.6 8.1 all-to-all-done
  105.0 15.2 %fusion.110 = bf16[4,16,2,1280]{3,1,2,0:T(8,128)(2,1)} fusion(bf16[4,1280,1280]{2,1,0:T(8,128)(2,1)} %get-tuple-element.499, bf16[16,1280,4,2]{1,0,3,2:T(8,128)(2,1)S(1)} %reshape.391, f32[4,1280]{1,0:T(4,128)S(1)} %divide_select_fusion.2), kind=kOutput, calls=%fused_computation.17.clone.1 | convolution fusion | flops 839516160 | bytes 13783040 | tf_op jit(solution)/shard_map/while/body/eval_jaxpr/rmnc,mln->rlmc/dot_general | solution.py:50
  134.1 6.2 all-to-all-done.1
  168.8 8.1 all-to-all-done
  181.1 15.2 %fusion.110 = bf16[4,16,2,1280]{3,1,2,0:T(8,128)(2,1)} fusion(bf16[4,1280,1280]{2,1,0:T(8,128)(2,1)} %get-tuple-element.499, bf16[16,1280,4,2]{1,0,3,2:T(8,128)(2,1)S(1)} %reshape.391, f32[4,1280]{1,0:T(4,128)S(1)} %divide_select_fusion.2), kind=kOutput, calls=%fused_computation.17.clone.1 | convolution fusion | flops 839516160 | bytes 13783040 | tf_op jit(solution)/shard_map/while/body/eval_jaxpr/rmnc,mln->rlmc/dot_general | solution.py:50
  244.9 8.1 all-to-all-done
  257.2 15.2 %fusion.110 = bf16[4,16,2,1280]{3,1,2,0:T(8,128)(2,1)} fusion(bf16[4,1280,1280]{2,1,0:T(8,128)(2,1)} %get-tuple-element.499, bf16[16,1280,4,2]{1,0,3,2:T(8,128)(2,1)S(1)} %reshape.391, f32[4,1280]{1,0:T(4,128)S(1)} %divide_select_fusion.2), kind=kOutput, calls=%fused_computation.17.clone.1 | convolution fusion | flops 839516160 | bytes 13783040 | tf_op jit(solution)/shard_map/while/body/eval_jaxpr/rmnc,mln->rlmc/dot_general | solution.py:50
  321.0 8.1 all-to-all-done
  333.3 15.2 %fusion.110 = bf16[4,16,2,1280]{3,1,2,0:T(8,128)(2,1)} fusion(bf16[4,1280,1280]{2,1,0:T(8,128)(2,1)} %get-tuple-element.499, bf16[16,1280,4,2]{1,0,3,2:T(8,128)(2,1)S(1)} %reshape.391, f32[4,1280]{1,0:T(4,128)S(1)} %divide_select_fusion.2), kind=kOutput, calls=%fused_computation.17.clone.1 | convolution fusion | flops 839516160 | bytes 13783040 | tf_op jit(solution)/shard_map/while/body/eval_jaxpr/rmnc,mln->rlmc/dot_general | solution.py:50
  362.4 6.2 all-to-all-done.1
  397.1 8.1 all-to-all-done
  409.4 15.2 %fusion.110 = bf16[4,16,2,1280]{3,1,2,0:T(8,128)(2,1)} fusion(bf16[4,1280,1280]{2,1,0:T(8,128)(2,1)} %get-tuple-element.499, bf16[16,1280,4,2]{1,0,3,2:T(8,128)(2,1)S(1)} %reshape.391, f32[4,1280]{1,0:T(4,128)S(1)} %divide_select_fusion.2), kind=kOutput, calls=%fused_computation.17.clone.1 | convolution fusion | flops 839516160 | bytes 13783040 | tf_op jit(solution)/shard_map/while/body/eval_jaxpr/rmnc,mln->rlmc/dot_general | solution.py:50
  438.5 6.2 all-to-all-done.1
  473.2 8.1 all-to-all-done
  485.5 15.2 %fusion.110 = bf16[4,16,2,1280]{3,1,2,0:T(8,128)(2,1)} fusion(bf16[4,1280,1280]{2,1,0:T(8,128)(2,1)} %get-tuple-element.499, bf16[16,1280,4,2]{1,0,3,2:T(8,128)(2,1)S(1)} %reshape.391, f32[4,1280]{1,0:T(4,128)S(1)} %divide_select_fusion.2), kind=kOutput, calls=%fused_computation.17.clone.1 | convolution fusion | flops 839516160 | bytes 13783040 | tf_op jit(solution)/shard_map/while/body/eval_jaxpr/rmnc,mln->rlmc/dot_general | solution.py:50
  514.6 6.2 all-to-all-done.1
  549.3 8.1 all-to-all-done
  561.6 15.2 %fusion.110 = bf16[4,16,2,1280]{3,1,2,0:T(8,128)(2,1)} fusion(bf16[4,1280,1280]{2,1,0:T(8,128)(2,1)} %get-tuple-element.499, bf16[16,1280,4,2]{1,0,3,2:T(8,128)(2,1)S(1)} %reshape.391, f32[4,1280]{1,0:T(4,128)S(1)} %divide_select_fusion.2), kind=kOutput, calls=%fused_computation.17.clone.1 | convolution fusion | flops 839516160 | bytes 13783040 | tf_op jit(solution)/shard_map/while/body/eval_jaxpr/rmnc,mln->rlmc/dot_general | solution.py:50
  590.7 6.2 all-to-all-done.1
  625.4 8.1 all-to-all-done
  637.7 15.2 %fusion.110 = bf16[4,16,2,1280]{3,1,2,0:T(8,128)(2,1)} fusion(bf16[4,1280,1280]{2,1,0:T(8,128)(2,1)} %get-tuple-element.499, bf16[16,1280,4,2]{1,0,3,2:T(8,128)(2,1)S(1)} %reshape.391, f32[4,1280]{1,0:T(4,128)S(1)} %divide_select_fusion.2), kind=kOutput, calls=%fused_computation.17.clone.1 | convolution fusion | flops 839516160 | bytes 13783040 | tf_op jit(solution)/shard_map/while/body/eval_jaxpr/rmnc,mln->rlmc/dot_general | solution.py:50
  701.5 8.1 all-to-all-done
  713.8 15.2 %fusion.110 = bf16[4,16,2,1280]{3,1,2,0:T(8,128)(2,1)} fusion(bf16[4,1280,1280]{2,1,0:T(8,128)(2,1)} %get-tuple-element.499, bf16[16,1280,4,2]{1,0,3,2:T(8,128)(2,1)S(1)} %reshape.391, f32[4,1280]{1,0:T(4,128)S(1)} %divide_select_fusion.2), kind=kOutput, calls=%fused_computation.17.clone.1 | convolution fusion | flops 839516160 | bytes 13783040 | tf_op jit(solution)/shard_map/while/body/eval_jaxpr/rmnc,mln->rlmc/dot_general | solution.py:50
  777.6 8.1 all-to-all-done
  789.9 15.2 %fusion.110 = bf16[4,16,2,1280]{3,1,2,0:T(8,128)(2,1)} fusion(bf16[4,1280,1280]{2,1,0:T(8,128)(2,1)} %get-tuple-element.499, bf16[16,1280,4,2]{1,0,3,2:T(8,128)(2,1)S(1)} %reshape.391, f32[4,1280]{1,0:T(4,128)S(1)} %divide_select_fusion.2), kind=kOutput, calls=%fused_computation.17.clone.1 | convolution fusion | flops 839516160 | bytes 13783040 | tf_op jit(solution)/shard_map/while/body/eval_jaxpr/rmnc,mln->rlmc/dot_general | solution.py:50
  819.0 6.2 all-to-all-done.1
  853.7 8.1 all-to-all-done
  866.0 15.2 %fusion.110 = bf16[4,16,2,1280]{3,1,2,0:T(8,128)(2,1)} fusion(bf16[4,1280,1280]{2,1,0:T(8,128)(2,1)} %get-tuple-element.499, bf16[16,1280,4,2]{1,0,3,2:T(8,128)(2,1)S(1)} %reshape.391, f32[4,1280]{1,0:T(4,128)S(1)} %divide_select_fusion.2), kind=kOutput, calls=%fused_computation.17.clone.1 | convolution fusion | flops 839516160 | bytes 13783040 | tf_op jit(solution)/shard_map/while/body/eval_jaxpr/rmnc,mln->rlmc/dot_general | solution.py:50
  934.2 169.7 %while.28 = (s32[]{:T(128)}, f32[1,32,1440]{2,1,0:T(8,128)S(1)}, bf16[12,1,32,1440]{3,2,1,0:T(8,128)(2,1)S(1)}, f32[1,4]{1,0:T(1,128)S(1)}, bf16[12,1,32,256]{3,...) while((s32[]{:T(128)}, f32[1,32,1440]{2,1,0:T(8,128)S(1)}, ...), condition=%wide.region_3.4_spmd, body=%wide.region_2.3_spmd.sunk | while | flops 24514560 | bytes 2624629 | solution.py:161
  934.9 9.9 all_gather.4
  949.0 10.5 all_gather.4
  963.7 9.3 all_gather.4
  977.3 9.6 all_gather.4
  991.1 9.6 all_gather.4
  1005.0 10.4 all_gather.4
  1019.6 9.6 all_gather.4
  1033.5 10.5 all_gather.4
  1048.2 9.3 all_gather.4
  1061.7 9.7 all_gather.4
  1075.6 9.6 all_gather.4
  1089.5 10.9 all_gather.4
  1104.4 39.4 %collective-permute-start.2 = (bf16[12,1,32,256]{3,2,0,1:T(8,128)(2,1)S(1)}, bf16[12,1,32,256]{3,2,0,1:T(8,128)(2,1)S(1)}, u32[]{:S(2)}, u32[]{:S(2)}) collective-permute-start(bf16[12,1,32,256]{3,2,0,1:T(8,128)(2,1)S(1)} %fusion.46), channel_id=1, source_target_pairs={{0,4},{4,8},{8,12},{12,16},{16,20},{20,24},{24,28},{28,32},{32,36}... | collective-permute-start | bytes 589832 | tf_op jit(solution)/shard_map/ppermute | solution.py:22
  1146.4 6.5 collective-permute-done.3
  (397 shorter events, 653.0 us)
Async XLA Ops:
  0.6 2.4 copy-start.4
  0.6 2.6 copy-start.12
  0.7 2.6 copy-start.8
  3.0 1.1 copy-start.5
  4.1 926.1 %copy-start.6 = (f32[4,4]{1,0:T(4,128)S(1)}, f32[4,4]{1,0:T(4,128)}, u32[]{:S(2)}) copy-start(f32[4,4]{1,0:T(4,128)} %param.30) | copy-start | bytes 196
  4.1 926.2 %copy-start.9 = (s32[32]{0:T(128)S(1)}, s32[32]{0:T(128)}, u32[]{:S(2)}) copy-start(s32[32]{0:T(128)} %param.32) | copy-start | bytes 388
  4.1 926.2 %copy-start.10 = (f32[32]{0:T(128)S(1)}, f32[32]{0:T(128)}, u32[]{:S(2)}) copy-start(f32[32]{0:T(128)} %param.33) | copy-start | bytes 388
  7.8 16.8 %all-to-all-start = ((bf16[32,2,2560]{2,1,0:T(2,128)(2,1)}), bf16[32,2,2560]{2,1,0:T(2,128)(2,1)S(1)}, u32[]{:S(2)}, u32[]{:S(2)}) async-start(bf16[32,2,2560]{2,1,0:T(2,128)(2,1)} %reshape.389), calls=%async_computation | async-start | bytes 655360 | tf_op jit(solution)/shard_map/while/body/eval_jaxpr/all_to_all | solution.py:98
  50.2 14.1 %all-to-all-start.1 = ((bf16[32,2,2560]{2,1,0:T(2,128)(2,1)}), bf16[32,2,2560]{2,1,0:T(2,128)(2,1)}, u32[]{:S(2)}, u32[]{:S(2)}) async-start(bf16[32,2,2560]{2,1,0:T(2,128)(2,1)} %reshape.392), calls=%async_computation.1 | async-start | bytes 655360 | tf_op jit(solution)/shard_map/while/body/eval_jaxpr/all_to_all | solution.py:100
  78.8 1.0 copy-start
  87.4 13.4 %all-to-all-start = ((bf16[32,2,2560]{2,1,0:T(2,128)(2,1)}), bf16[32,2,2560]{2,1,0:T(2,128)(2,1)S(1)}, u32[]{:S(2)}, u32[]{:S(2)}) async-start(bf16[32,2,2560]{2,1,0:T(2,128)(2,1)} %reshape.389), calls=%async_computation | async-start | bytes 655360 | tf_op jit(solution)/shard_map/while/body/eval_jaxpr/all_to_all | solution.py:98
  126.3 14.1 %all-to-all-start.1 = ((bf16[32,2,2560]{2,1,0:T(2,128)(2,1)}), bf16[32,2,2560]{2,1,0:T(2,128)(2,1)}, u32[]{:S(2)}, u32[]{:S(2)}) async-start(bf16[32,2,2560]{2,1,0:T(2,128)(2,1)} %reshape.392), calls=%async_computation.1 | async-start | bytes 655360 | tf_op jit(solution)/shard_map/while/body/eval_jaxpr/all_to_all | solution.py:100
  154.9 1.0 copy-start
  163.5 13.4 %all-to-all-start = ((bf16[32,2,2560]{2,1,0:T(2,128)(2,1)}), bf16[32,2,2560]{2,1,0:T(2,128)(2,1)S(1)}, u32[]{:S(2)}, u32[]{:S(2)}) async-start(bf16[32,2,2560]{2,1,0:T(2,128)(2,1)} %reshape.389), calls=%async_computation | async-start | bytes 655360 | tf_op jit(solution)/shard_map/while/body/eval_jaxpr/all_to_all | solution.py:98
  202.4 14.1 %all-to-all-start.1 = ((bf16[32,2,2560]{2,1,0:T(2,128)(2,1)}), bf16[32,2,2560]{2,1,0:T(2,128)(2,1)}, u32[]{:S(2)}, u32[]{:S(2)}) async-start(bf16[32,2,2560]{2,1,0:T(2,128)(2,1)} %reshape.392), calls=%async_computation.1 | async-start | bytes 655360 | tf_op jit(solution)/shard_map/while/body/eval_jaxpr/all_to_all | solution.py:100
  239.6 13.4 %all-to-all-start = ((bf16[32,2,2560]{2,1,0:T(2,128)(2,1)}), bf16[32,2,2560]{2,1,0:T(2,128)(2,1)S(1)}, u32[]{:S(2)}, u32[]{:S(2)}) async-start(bf16[32,2,2560]{2,1,0:T(2,128)(2,1)} %reshape.389), calls=%async_computation | async-start | bytes 655360 | tf_op jit(solution)/shard_map/while/body/eval_jaxpr/all_to_all | solution.py:98
  278.5 14.1 %all-to-all-start.1 = ((bf16[32,2,2560]{2,1,0:T(2,128)(2,1)}), bf16[32,2,2560]{2,1,0:T(2,128)(2,1)}, u32[]{:S(2)}, u32[]{:S(2)}) async-start(bf16[32,2,2560]{2,1,0:T(2,128)(2,1)} %reshape.392), calls=%async_computation.1 | async-start | bytes 655360 | tf_op jit(solution)/shard_map/while/body/eval_jaxpr/all_to_all | solution.py:100
  307.1 1.0 copy-start
  315.7 13.4 %all-to-all-start = ((bf16[32,2,2560]{2,1,0:T(2,128)(2,1)}), bf16[32,2,2560]{2,1,0:T(2,128)(2,1)S(1)}, u32[]{:S(2)}, u32[]{:S(2)}) async-start(bf16[32,2,2560]{2,1,0:T(2,128)(2,1)} %reshape.389), calls=%async_computation | async-start | bytes 655360 | tf_op jit(solution)/shard_map/while/body/eval_jaxpr/all_to_all | solution.py:98
  354.6 14.1 %all-to-all-start.1 = ((bf16[32,2,2560]{2,1,0:T(2,128)(2,1)}), bf16[32,2,2560]{2,1,0:T(2,128)(2,1)}, u32[]{:S(2)}, u32[]{:S(2)}) async-start(bf16[32,2,2560]{2,1,0:T(2,128)(2,1)} %reshape.392), calls=%async_computation.1 | async-start | bytes 655360 | tf_op jit(solution)/shard_map/while/body/eval_jaxpr/all_to_all | solution.py:100
  391.8 13.4 %all-to-all-start = ((bf16[32,2,2560]{2,1,0:T(2,128)(2,1)}), bf16[32,2,2560]{2,1,0:T(2,128)(2,1)S(1)}, u32[]{:S(2)}, u32[]{:S(2)}) async-start(bf16[32,2,2560]{2,1,0:T(2,128)(2,1)} %reshape.389), calls=%async_computation | async-start | bytes 655360 | tf_op jit(solution)/shard_map/while/body/eval_jaxpr/all_to_all | solution.py:98
  430.7 14.1 %all-to-all-start.1 = ((bf16[32,2,2560]{2,1,0:T(2,128)(2,1)}), bf16[32,2,2560]{2,1,0:T(2,128)(2,1)}, u32[]{:S(2)}, u32[]{:S(2)}) async-start(bf16[32,2,2560]{2,1,0:T(2,128)(2,1)} %reshape.392), calls=%async_computation.1 | async-start | bytes 655360 | tf_op jit(solution)/shard_map/while/body/eval_jaxpr/all_to_all | solution.py:100
  467.9 13.4 %all-to-all-start = ((bf16[32,2,2560]{2,1,0:T(2,128)(2,1)}), bf16[32,2,2560]{2,1,0:T(2,128)(2,1)S(1)}, u32[]{:S(2)}, u32[]{:S(2)}) async-start(bf16[32,2,2560]{2,1,0:T(2,128)(2,1)} %reshape.389), calls=%async_computation | async-start | bytes 655360 | tf_op jit(solution)/shard_map/while/body/eval_jaxpr/all_to_all | solution.py:98
  506.8 14.1 %all-to-all-start.1 = ((bf16[32,2,2560]{2,1,0:T(2,128)(2,1)}), bf16[32,2,2560]{2,1,0:T(2,128)(2,1)}, u32[]{:S(2)}, u32[]{:S(2)}) async-start(bf16[32,2,2560]{2,1,0:T(2,128)(2,1)} %reshape.392), calls=%async_computation.1 | async-start | bytes 655360 | tf_op jit(solution)/shard_map/while/body/eval_jaxpr/all_to_all | solution.py:100
  535.4 1.0 copy-start
  544.0 13.4 %all-to-all-start = ((bf16[32,2,2560]{2,1,0:T(2,128)(2,1)}), bf16[32,2,2560]{2,1,0:T(2,128)(2,1)S(1)}, u32[]{:S(2)}, u32[]{:S(2)}) async-start(bf16[32,2,2560]{2,1,0:T(2,128)(2,1)} %reshape.389), calls=%async_computation | async-start | bytes 655360 | tf_op jit(solution)/shard_map/while/body/eval_jaxpr/all_to_all | solution.py:98
  582.9 14.1 %all-to-all-start.1 = ((bf16[32,2,2560]{2,1,0:T(2,128)(2,1)}), bf16[32,2,2560]{2,1,0:T(2,128)(2,1)}, u32[]{:S(2)}, u32[]{:S(2)}) async-start(bf16[32,2,2560]{2,1,0:T(2,128)(2,1)} %reshape.392), calls=%async_computation.1 | async-start | bytes 655360 | tf_op jit(solution)/shard_map/while/body/eval_jaxpr/all_to_all | solution.py:100
  611.5 1.0 copy-start
  620.1 13.4 %all-to-all-start = ((bf16[32,2,2560]{2,1,0:T(2,128)(2,1)}), bf16[32,2,2560]{2,1,0:T(2,128)(2,1)S(1)}, u32[]{:S(2)}, u32[]{:S(2)}) async-start(bf16[32,2,2560]{2,1,0:T(2,128)(2,1)} %reshape.389), calls=%async_computation | async-start | bytes 655360 | tf_op jit(solution)/shard_map/while/body/eval_jaxpr/all_to_all | solution.py:98
  659.0 14.1 %all-to-all-start.1 = ((bf16[32,2,2560]{2,1,0:T(2,128)(2,1)}), bf16[32,2,2560]{2,1,0:T(2,128)(2,1)}, u32[]{:S(2)}, u32[]{:S(2)}) async-start(bf16[32,2,2560]{2,1,0:T(2,128)(2,1)} %reshape.392), calls=%async_computation.1 | async-start | bytes 655360 | tf_op jit(solution)/shard_map/while/body/eval_jaxpr/all_to_all | solution.py:100
  687.7 1.0 copy-start
  696.3 13.4 %all-to-all-start = ((bf16[32,2,2560]{2,1,0:T(2,128)(2,1)}), bf16[32,2,2560]{2,1,0:T(2,128)(2,1)S(1)}, u32[]{:S(2)}, u32[]{:S(2)}) async-start(bf16[32,2,2560]{2,1,0:T(2,128)(2,1)} %reshape.389), calls=%async_computation | async-start | bytes 655360 | tf_op jit(solution)/shard_map/while/body/eval_jaxpr/all_to_all | solution.py:98
  735.1 14.1 %all-to-all-start.1 = ((bf16[32,2,2560]{2,1,0:T(2,128)(2,1)}), bf16[32,2,2560]{2,1,0:T(2,128)(2,1)}, u32[]{:S(2)}, u32[]{:S(2)}) async-start(bf16[32,2,2560]{2,1,0:T(2,128)(2,1)} %reshape.392), calls=%async_computation.1 | async-start | bytes 655360 | tf_op jit(solution)/shard_map/while/body/eval_jaxpr/all_to_all | solution.py:100
  763.8 1.0 copy-start
  772.4 13.4 %all-to-all-start = ((bf16[32,2,2560]{2,1,0:T(2,128)(2,1)}), bf16[32,2,2560]{2,1,0:T(2,128)(2,1)S(1)}, u32[]{:S(2)}, u32[]{:S(2)}) async-start(bf16[32,2,2560]{2,1,0:T(2,128)(2,1)} %reshape.389), calls=%async_computation | async-start | bytes 655360 | tf_op jit(solution)/shard_map/while/body/eval_jaxpr/all_to_all | solution.py:98
  811.2 14.1 %all-to-all-start.1 = ((bf16[32,2,2560]{2,1,0:T(2,128)(2,1)}), bf16[32,2,2560]{2,1,0:T(2,128)(2,1)}, u32[]{:S(2)}, u32[]{:S(2)}) async-start(bf16[32,2,2560]{2,1,0:T(2,128)(2,1)} %reshape.392), calls=%async_computation.1 | async-start | bytes 655360 | tf_op jit(solution)/shard_map/while/body/eval_jaxpr/all_to_all | solution.py:100
  848.5 13.4 %all-to-all-start = ((bf16[32,2,2560]{2,1,0:T(2,128)(2,1)}), bf16[32,2,2560]{2,1,0:T(2,128)(2,1)S(1)}, u32[]{:S(2)}, u32[]{:S(2)}) async-start(bf16[32,2,2560]{2,1,0:T(2,128)(2,1)} %reshape.389), calls=%async_computation | async-start | bytes 655360 | tf_op jit(solution)/shard_map/while/body/eval_jaxpr/all_to_all | solution.py:98
  887.3 14.1 %all-to-all-start.1 = ((bf16[32,2,2560]{2,1,0:T(2,128)(2,1)}), bf16[32,2,2560]{2,1,0:T(2,128)(2,1)}, u32[]{:S(2)}, u32[]{:S(2)}) async-start(bf16[32,2,2560]{2,1,0:T(2,128)(2,1)} %reshape.392), calls=%async_computation.1 | async-start | bytes 655360 | tf_op jit(solution)/shard_map/while/body/eval_jaxpr/all_to_all | solution.py:100
  921.0 9.4 copy-start.7
  921.1 12.2 %collective-permute-start = (bf16[12,1,8,256]{3,2,0,1:T(8,128)(2,1)S(1)}, bf16[12,1,8,256]{3,2,0,1:T(8,128)(2,1)S(1)}, u32[]{:S(2)}, u32[]{:S(2)}) collective-permute-start(bf16[12,1,8,256]{3,2,0,1:T(8,128)(2,1)S(1)} %get-tuple-element.349), channel_id=1, source_target_pairs={{0,4},{4,8},{8,12},{12,16},{16,20},{20,24},{24,28},{28,32},{32,36}... | collective-permute-start | bytes 147464 | tf_op jit(solution)/shard_map/ppermute | solution.py:22
  924.3 9.0 collective-permute-start.1
  932.0 2.2 copy-start.2
  932.0 2.2 copy-start.3
  932.0 2.2 copy-start.11
  1103.9 50.1 %copy-start.1 = (f32[1,32,1440]{2,1,0:T(8,128)}, f32[1,32,1440]{2,1,0:T(8,128)S(1)}, u32[]{:S(2)}) copy-start(f32[1,32,1440]{2,1,0:T(8,128)S(1)} %get-tuple-element.305) | copy-start | bytes 552964
  1103.9 41.8 %copy-start.13 = (f32[40]{0:T(128)S(1)}, f32[40]{0:T(128)}, u32[]{:S(2)}) copy-start(f32[40]{0:T(128)} %param.35) | copy-start | bytes 484
  1104.4 42.0 %collective-permute-start.2 = (bf16[12,1,32,256]{3,2,0,1:T(8,128)(2,1)S(1)}, bf16[12,1,32,256]{3,2,0,1:T(8,128)(2,1)S(1)}, u32[]{:S(2)}, u32[]{:S(2)}) collective-permute-start(bf16[12,1,32,256]{3,2,0,1:T(8,128)(2,1)S(1)} %fusion.46), channel_id=1, source_target_pairs={{0,4},{4,8},{8,12},{12,16},{16,20},{20,24},{24,28},{28,32},{32,36}... | collective-permute-start | bytes 589832 | tf_op jit(solution)/shard_map/ppermute | solution.py:22
  1143.8 9.1 collective-permute-start.3
  (5 other events, 4.9 us)
where the time goes:
time: 1160 us; the launch traced here: 1150 us
  local copies, waits for them, and re-layouts  398 us (34%)
  matrix products  238 us (21%)
  starting transfers between devices  181 us (16%)
  waiting for transfers between devices  180 us (16%)
  blocking collectives  119 us (10%)
  other arithmetic  34.7 us (3%)
    dot_general x12, matrix products, padded_transform(): jnp.einsum('rmnc,mln->rlmc', damped, tables, preferred_element_type=jnp.f...  182 us
    while x84, local copies, waits for them, and re-layouts  153 us
    all_gather x12, blocking collectives, ocean_advance(): lax.all_gather(ocean_now.astype(jnp.bfloat16), 'lev', axis=0, tiled=True)  119 us
    convert_element_type x36, local copies, waits for them, and re-layouts, march_air_model(): synthesis_field = returned.reshape(field_local, height_pile, lat_local, c...  108 us
    all_to_all x12, waiting for transfers between devices, march_air_model(): lax.all_to_all(scaled, 'band', split_axis=2, concat_axis=1, tiled=True)  97.5 us
    all_to_all x12, waiting for transfers between devices, march_air_model(): lax.all_to_all(synthesis, 'band', split_axis=1, concat_axis=2, tiled=True)  74.9 us
    all_to_all x12, starting transfers between devices, march_air_model(): lax.all_to_all(synthesis, 'band', split_axis=1, concat_axis=2, tiled=True)  69.3 us
    all_to_all x12, starting transfers between devices, march_air_model(): lax.all_to_all(scaled, 'band', split_axis=2, concat_axis=1, tiled=True)  65.2 us
  transfers between devices with their start and end apart: 28, of which 26 were waited for; matrix products, arithmetic and copies ran while one was open for 3% of the time, Pallas kernels for 0%

commit v1 on v0

--- a/solution.py
+++ b/solution.py
@@ -97,7 +97,10 @@
         scaled = scaled.reshape(row_count, lat_local, column_count)
         by_wave = lax.all_to_all(scaled, "band", split_axis=2, concat_axis=1, tiled=True)
         synthesis = transform(by_wave)
-        returned = lax.all_to_all(synthesis, "band", split_axis=1, concat_axis=2, tiled=True)
+        peers = lax.axis_size("band")
+        blocks = jnp.stack(jnp.split(synthesis, peers, axis=1), axis=0)
+        blocks = lax.all_to_all(blocks, "band", split_axis=0, concat_axis=0)
+        returned = jnp.concatenate(blocks, axis=2)
         synthesis_field = returned.reshape(
             field_local, height_pile, lat_local, column_count
         ).astype(jnp.float32)

time: 1160 us -> 1000 us (0.86)
  local copies, waits for them, and re-layouts: 398 us -> 238 us
  matrix products: 238 us -> 220 us
  other arithmetic: 34.7 us -> 49.4 us
    convert_element_type x36 -> x12, local copies, waits for them, and re-layouts: 108 us -> 22.5 us  [march_air_model(): synthesis_field = returned.reshape(field_local, height_pile, lat_local, c...]
    reshape x12 -> x0, local copies, waits for them, and re-layouts: 31.7 us -> none  [padded_transform(): synthesis.astype(jnp.bfloat16).reshape(row_count, lat_count, wave_count * 2)]
    while x84 -> x480, local copies, waits for them, and re-layouts: 153 us -> 125 us
    all_to_all x12 -> x0, local copies, waits for them, and re-layouts: 28.3 us -> none  [march_air_model(): lax.all_to_all(synthesis, 'band', split_axis=1, concat_axis=2, tiled=True)]
    sub x12, other arithmetic: 10.8 us -> 23.9 us  [march_air_model(): halfway_point = air_model_present - synthesis_field]
  transfers between devices with their start and end apart: 28 -> 28, of which waited for: 26 -> 26; matrix products, arithmetic and copies ran while one was open for 3% -> 2% of each run, Pallas kernels for 0% -> 0%
where the time goes in v1:
time: 1000 us; the launch traced here: 996 us
  local copies, waits for them, and re-layouts  238 us (24%)
  matrix products  220 us (22%)
  waiting for transfers between devices  191 us (19%)
  starting transfers between devices  172 us (17%)
  blocking collectives  121 us (12%)
  other arithmetic  49.4 us (5%)
    dot_general x12, matrix products, padded_transform(): jnp.einsum('rmnc,mln->rlmc', damped, tables, preferred_element_type=jnp.f...  173 us
    while x480, local copies, waits for them, and re-layouts  125 us
    all_gather x12, blocking collectives, ocean_advance(): lax.all_gather(ocean_now.astype(jnp.bfloat16), 'lev', axis=0, tiled=True)  121 us
    all_to_all x12, waiting for transfers between devices, march_air_model(): lax.all_to_all(scaled, 'band', split_axis=2, concat_axis=1, tiled=True)  97.5 us
    all_to_all x12, waiting for transfers between devices, march_air_model(): blocks = lax.all_to_all(blocks, 'band', split_axis=0, concat_axis=0)  86.5 us
    all_to_all x12, starting transfers between devices, march_air_model(): lax.all_to_all(scaled, 'band', split_axis=2, concat_axis=1, tiled=True)  65.2 us
    all_to_all x12, starting transfers between devices, march_air_model(): blocks = lax.all_to_all(blocks, 'band', split_axis=0, concat_axis=0)  61.6 us
    ppermute x2, starting transfers between devices, with_halo(): before = lax.ppermute(last, axis, up)  41.3 us
  transfers between devices with their start and end apart: 28, of which 26 were waited for; matrix products, arithmetic and copies ran while one was open for 2% of the time, Pallas kernels for 0%

profile of v1, /device:TPU:15, one launch (start us, length us, event | category | flops | bytes accessed | tf_op | source)
XLA Modules:
  0.0 996.5 jit_solution(5319033591037402079)
XLA Ops:
  4.0 767.4 %while.29 = (s32[]{:T(128)}, f32[1,16,40,256]{3,1,2,0:T(8,128)S(1)}, bf16[12,1,40,256]{3,2,1,0:T(8,128)(2,1)}, f32[40]{0:T(128)S(1)}, bf16[4,1280,1280]{2,1,0:T(...) while((s32[]{:T(128)}, ...), condition=%wide.region_1.2_spmd.clone, body=%wide.region_0.1_spmd.clone.sunk | while | flops 871715840 | bytes 35641944 | solution.py:117
  8.5 8.7 all-to-all-start
  17.3 8.1 all-to-all-done
  29.6 14.4 %fusion.114 = bf16[4,16,2,1280]{3,1,2,0:T(8,128)(2,1)S(1)} fusion(bf16[4,1280,1280]{2,1,0:T(8,128)(2,1)} %get-tuple-element.557, bf16[16,1280,4,2]{1,0,3,2:T(8,128)(2,1)S(1)} %reshape.389, f32[4,1280]{1,0:T(4,128)S(1)} %divide_select_fusion.2), kind=kOutput, calls=%fused_computation.17.clone.1 | convolution fusion | flops 839516160 | bytes 13783040 | tf_op jit(solution)/shard_map/while/body/eval_jaxpr/rmnc,mln->rlmc/dot_general | solution.py:50
  53.7 7.2 all-to-all-done.1
  80.9 8.1 all-to-all-done
  93.2 14.4 %fusion.114 = bf16[4,16,2,1280]{3,1,2,0:T(8,128)(2,1)S(1)} fusion(bf16[4,1280,1280]{2,1,0:T(8,128)(2,1)} %get-tuple-element.557, bf16[16,1280,4,2]{1,0,3,2:T(8,128)(2,1)S(1)} %reshape.389, f32[4,1280]{1,0:T(4,128)S(1)} %divide_select_fusion.2), kind=kOutput, calls=%fused_computation.17.clone.1 | convolution fusion | flops 839516160 | bytes 13783040 | tf_op jit(solution)/shard_map/while/body/eval_jaxpr/rmnc,mln->rlmc/dot_general | solution.py:50
  117.4 7.2 all-to-all-done.1
  144.5 8.1 all-to-all-done
  156.9 14.4 %fusion.114 = bf16[4,16,2,1280]{3,1,2,0:T(8,128)(2,1)S(1)} fusion(bf16[4,1280,1280]{2,1,0:T(8,128)(2,1)} %get-tuple-element.557, bf16[16,1280,4,2]{1,0,3,2:T(8,128)(2,1)S(1)} %reshape.389, f32[4,1280]{1,0:T(4,128)S(1)} %divide_select_fusion.2), kind=kOutput, calls=%fused_computation.17.clone.1 | convolution fusion | flops 839516160 | bytes 13783040 | tf_op jit(solution)/shard_map/while/body/eval_jaxpr/rmnc,mln->rlmc/dot_general | solution.py:50
  181.0 7.2 all-to-all-done.1
  208.2 8.1 all-to-all-done
  220.5 14.4 %fusion.114 = bf16[4,16,2,1280]{3,1,2,0:T(8,128)(2,1)S(1)} fusion(bf16[4,1280,1280]{2,1,0:T(8,128)(2,1)} %get-tuple-element.557, bf16[16,1280,4,2]{1,0,3,2:T(8,128)(2,1)S(1)} %reshape.389, f32[4,1280]{1,0:T(4,128)S(1)} %divide_select_fusion.2), kind=kOutput, calls=%fused_computation.17.clone.1 | convolution fusion | flops 839516160 | bytes 13783040 | tf_op jit(solution)/shard_map/while/body/eval_jaxpr/rmnc,mln->rlmc/dot_general | solution.py:50
  244.6 7.2 all-to-all-done.1
  271.8 8.1 all-to-all-done
  284.1 14.4 %fusion.114 = bf16[4,16,2,1280]{3,1,2,0:T(8,128)(2,1)S(1)} fusion(bf16[4,1280,1280]{2,1,0:T(8,128)(2,1)} %get-tuple-element.557, bf16[16,1280,4,2]{1,0,3,2:T(8,128)(2,1)S(1)} %reshape.389, f32[4,1280]{1,0:T(4,128)S(1)} %divide_select_fusion.2), kind=kOutput, calls=%fused_computation.17.clone.1 | convolution fusion | flops 839516160 | bytes 13783040 | tf_op jit(solution)/shard_map/while/body/eval_jaxpr/rmnc,mln->rlmc/dot_general | solution.py:50
  308.3 7.2 all-to-all-done.1
  335.5 8.1 all-to-all-done
  347.8 14.4 %fusion.114 = bf16[4,16,2,1280]{3,1,2,0:T(8,128)(2,1)S(1)} fusion(bf16[4,1280,1280]{2,1,0:T(8,128)(2,1)} %get-tuple-element.557, bf16[16,1280,4,2]{1,0,3,2:T(8,128)(2,1)S(1)} %reshape.389, f32[4,1280]{1,0:T(4,128)S(1)} %divide_select_fusion.2), kind=kOutput, calls=%fused_computation.17.clone.1 | convolution fusion | flops 839516160 | bytes 13783040 | tf_op jit(solution)/shard_map/while/body/eval_jaxpr/rmnc,mln->rlmc/dot_general | solution.py:50
  371.9 7.2 all-to-all-done.1
  399.1 8.1 all-to-all-done
  411.4 14.4 %fusion.114 = bf16[4,16,2,1280]{3,1,2,0:T(8,128)(2,1)S(1)} fusion(bf16[4,1280,1280]{2,1,0:T(8,128)(2,1)} %get-tuple-element.557, bf16[16,1280,4,2]{1,0,3,2:T(8,128)(2,1)S(1)} %reshape.389, f32[4,1280]{1,0:T(4,128)S(1)} %divide_select_fusion.2), kind=kOutput, calls=%fused_computation.17.clone.1 | convolution fusion | flops 839516160 | bytes 13783040 | tf_op jit(solution)/shard_map/while/body/eval_jaxpr/rmnc,mln->rlmc/dot_general | solution.py:50
  435.6 7.2 all-to-all-done.1
  462.7 8.1 all-to-all-done
  475.1 14.4 %fusion.114 = bf16[4,16,2,1280]{3,1,2,0:T(8,128)(2,1)S(1)} fusion(bf16[4,1280,1280]{2,1,0:T(8,128)(2,1)} %get-tuple-element.557, bf16[16,1280,4,2]{1,0,3,2:T(8,128)(2,1)S(1)} %reshape.389, f32[4,1280]{1,0:T(4,128)S(1)} %divide_select_fusion.2), kind=kOutput, calls=%fused_computation.17.clone.1 | convolution fusion | flops 839516160 | bytes 13783040 | tf_op jit(solution)/shard_map/while/body/eval_jaxpr/rmnc,mln->rlmc/dot_general | solution.py:50
  499.2 7.2 all-to-all-done.1
  526.4 8.1 all-to-all-done
  538.7 14.4 %fusion.114 = bf16[4,16,2,1280]{3,1,2,0:T(8,128)(2,1)S(1)} fusion(bf16[4,1280,1280]{2,1,0:T(8,128)(2,1)} %get-tuple-element.557, bf16[16,1280,4,2]{1,0,3,2:T(8,128)(2,1)S(1)} %reshape.389, f32[4,1280]{1,0:T(4,128)S(1)} %divide_select_fusion.2), kind=kOutput, calls=%fused_computation.17.clone.1 | convolution fusion | flops 839516160 | bytes 13783040 | tf_op jit(solution)/shard_map/while/body/eval_jaxpr/rmnc,mln->rlmc/dot_general | solution.py:50
  590.0 8.1 all-to-all-done
  602.4 14.4 %fusion.114 = bf16[4,16,2,1280]{3,1,2,0:T(8,128)(2,1)S(1)} fusion(bf16[4,1280,1280]{2,1,0:T(8,128)(2,1)} %get-tuple-element.557, bf16[16,1280,4,2]{1,0,3,2:T(8,128)(2,1)S(1)} %reshape.389, f32[4,1280]{1,0:T(4,128)S(1)} %divide_select_fusion.2), kind=kOutput, calls=%fused_computation.17.clone.1 | convolution fusion | flops 839516160 | bytes 13783040 | tf_op jit(solution)/shard_map/while/body/eval_jaxpr/rmnc,mln->rlmc/dot_general | solution.py:50
  653.7 8.1 all-to-all-done
  666.0 14.4 %fusion.114 = bf16[4,16,2,1280]{3,1,2,0:T(8,128)(2,1)S(1)} fusion(bf16[4,1280,1280]{2,1,0:T(8,128)(2,1)} %get-tuple-element.557, bf16[16,1280,4,2]{1,0,3,2:T(8,128)(2,1)S(1)} %reshape.389, f32[4,1280]{1,0:T(4,128)S(1)} %divide_select_fusion.2), kind=kOutput, calls=%fused_computation.17.clone.1 | convolution fusion | flops 839516160 | bytes 13783040 | tf_op jit(solution)/shard_map/while/body/eval_jaxpr/rmnc,mln->rlmc/dot_general | solution.py:50
  717.3 8.1 all-to-all-done
  729.6 14.4 %fusion.114 = bf16[4,16,2,1280]{3,1,2,0:T(8,128)(2,1)S(1)} fusion(bf16[4,1280,1280]{2,1,0:T(8,128)(2,1)} %get-tuple-element.557, bf16[16,1280,4,2]{1,0,3,2:T(8,128)(2,1)S(1)} %reshape.389, f32[4,1280]{1,0:T(4,128)S(1)} %divide_select_fusion.2), kind=kOutput, calls=%fused_computation.17.clone.1 | convolution fusion | flops 839516160 | bytes 13783040 | tf_op jit(solution)/shard_map/while/body/eval_jaxpr/rmnc,mln->rlmc/dot_general | solution.py:50
  784.7 162.9 %while.28 = (s32[]{:T(128)}, f32[1,32,1440]{2,1,0:T(8,128)S(1)}, bf16[12,1,32,1440]{3,2,1,0:T(8,128)(2,1)S(1)}, f32[1,4]{1,0:T(1,128)S(1)}, bf16[12,1,32,256]{3,...) while((s32[]{:T(128)}, f32[1,32,1440]{2,1,0:T(8,128)S(1)}, ...), condition=%wide.region_3.4_spmd, body=%wide.region_2.3_spmd.sunk | while | flops 24514560 | bytes 2624629 | solution.py:164
  785.4 9.9 all_gather.4
  798.8 10.5 %all_gather.4 = bf16[4,32,1440]{2,1,0:T(8,128)(2,1)S(1)} all-gather(bf16[1,32,1440]{2,1,0:T(8,128)(2,1)S(1)} %convert_element_type.205), channel_id=1, replica_groups=mesh['band'=32,'lev'=4] {'lev'}, dimensions={0}, use_global_device_ids=true | all-gather | bytes 460800 | tf_op jit(solution)/shard_map/while/body/eval_jaxpr/all_gather | solution.py:151
  812.8 9.3 all_gather.4
  825.7 10.2 %all_gather.4 = bf16[4,32,1440]{2,1,0:T(8,128)(2,1)S(1)} all-gather(bf16[1,32,1440]{2,1,0:T(8,128)(2,1)S(1)} %convert_element_type.205), channel_id=1, replica_groups=mesh['band'=32,'lev'=4] {'lev'}, dimensions={0}, use_global_device_ids=true | all-gather | bytes 460800 | tf_op jit(solution)/shard_map/while/body/eval_jaxpr/all_gather | solution.py:151
  839.4 9.6 all_gather.4
  852.5 10.9 %all_gather.4 = bf16[4,32,1440]{2,1,0:T(8,128)(2,1)S(1)} all-gather(bf16[1,32,1440]{2,1,0:T(8,128)(2,1)S(1)} %convert_element_type.205), channel_id=1, replica_groups=mesh['band'=32,'lev'=4] {'lev'}, dimensions={0}, use_global_device_ids=true | all-gather | bytes 460800 | tf_op jit(solution)/shard_map/while/body/eval_jaxpr/all_gather | solution.py:151
  866.9 9.6 all_gather.4
  880.1 10.5 %all_gather.4 = bf16[4,32,1440]{2,1,0:T(8,128)(2,1)S(1)} all-gather(bf16[1,32,1440]{2,1,0:T(8,128)(2,1)S(1)} %convert_element_type.205), channel_id=1, replica_groups=mesh['band'=32,'lev'=4] {'lev'}, dimensions={0}, use_global_device_ids=true | all-gather | bytes 460800 | tf_op jit(solution)/shard_map/while/body/eval_jaxpr/all_gather | solution.py:151
  894.1 9.3 all_gather.4
  906.9 10.4 %all_gather.4 = bf16[4,32,1440]{2,1,0:T(8,128)(2,1)S(1)} all-gather(bf16[1,32,1440]{2,1,0:T(8,128)(2,1)S(1)} %convert_element_type.205), channel_id=1, replica_groups=mesh['band'=32,'lev'=4] {'lev'}, dimensions={0}, use_global_device_ids=true | all-gather | bytes 460800 | tf_op jit(solution)/shard_map/while/body/eval_jaxpr/all_gather | solution.py:151
  920.8 9.6 all_gather.4
  934.0 10.8 %all_gather.4 = bf16[4,32,1440]{2,1,0:T(8,128)(2,1)S(1)} all-gather(bf16[1,32,1440]{2,1,0:T(8,128)(2,1)S(1)} %convert_element_type.205), channel_id=1, replica_groups=mesh['band'=32,'lev'=4] {'lev'}, dimensions={0}, use_global_device_ids=true | all-gather | bytes 460800 | tf_op jit(solution)/shard_map/while/body/eval_jaxpr/all_gather | solution.py:151
  948.2 38.1 %collective-permute-start.2 = (bf16[12,1,32,256]{3,2,0,1:T(8,128)(2,1)S(1)}, bf16[12,1,32,256]{3,2,0,1:T(8,128)(2,1)S(1)}, u32[]{:S(2)}, u32[]{:S(2)}) collective-permute-start(bf16[12,1,32,256]{3,2,0,1:T(8,128)(2,1)S(1)} %fusion.46), channel_id=1, source_target_pairs={{0,4},{4,8},{8,12},{12,16},{16,20},{20,24},{24,28},{28,32},{32,36}... | collective-permute-start | bytes 589832 | tf_op jit(solution)/shard_map/ppermute | solution.py:22
  (797 shorter events, 494.5 us)
Async XLA Ops:
  0.6 2.6 copy-start.15
  0.7 2.6 copy-start.11
  4.0 777.3 %copy-start.9 = (f32[4,4]{1,0:T(4,128)S(1)}, f32[4,4]{1,0:T(4,128)}, u32[]{:S(2)}) copy-start(f32[4,4]{1,0:T(4,128)} %param.30) | copy-start | bytes 196
  4.0 777.4 %copy-start.12 = (s32[32]{0:T(128)S(1)}, s32[32]{0:T(128)}, u32[]{:S(2)}) copy-start(s32[32]{0:T(128)} %param.32) | copy-start | bytes 388
  4.0 777.4 %copy-start.13 = (f32[32]{0:T(128)S(1)}, f32[32]{0:T(128)}, u32[]{:S(2)}) copy-start(f32[32]{0:T(128)} %param.33) | copy-start | bytes 388
  8.5 16.8 %all-to-all-start = ((bf16[32,2,2560]{2,1,0:T(2,128)(2,1)}), bf16[32,2,2560]{2,1,0:T(2,128)(2,1)S(1)}, u32[]{:S(2)}, u32[]{:S(2)}) async-start(bf16[32,2,2560]{2,1,0:T(2,128)(2,1)} %reshape.387), calls=%async_computation | async-start | bytes 655360 | tf_op jit(solution)/shard_map/while/body/eval_jaxpr/all_to_all | solution.py:98
  47.6 13.4 %all-to-all-start.1 = ((bf16[32,2,2560]{2,1,0:T(2,128)(2,1)}), bf16[32,2,2560]{2,1,0:T(2,128)(2,1)S(1)}, u32[]{:S(2)}, u32[]{:S(2)}) async-start(bf16[32,2,2560]{2,1,0:T(2,128)(2,1)} %reshape.390), calls=%async_computation.1 | async-start | bytes 655360 | tf_op jit(solution)/shard_map/while/body/eval_jaxpr/all_to_all | solution.py:102
  66.6 4.5 copy-start.2
  75.7 13.4 %all-to-all-start = ((bf16[32,2,2560]{2,1,0:T(2,128)(2,1)}), bf16[32,2,2560]{2,1,0:T(2,128)(2,1)S(1)}, u32[]{:S(2)}, u32[]{:S(2)}) async-start(bf16[32,2,2560]{2,1,0:T(2,128)(2,1)} %reshape.387), calls=%async_computation | async-start | bytes 655360 | tf_op jit(solution)/shard_map/while/body/eval_jaxpr/all_to_all | solution.py:98
  111.2 13.4 %all-to-all-start.1 = ((bf16[32,2,2560]{2,1,0:T(2,128)(2,1)}), bf16[32,2,2560]{2,1,0:T(2,128)(2,1)S(1)}, u32[]{:S(2)}, u32[]{:S(2)}) async-start(bf16[32,2,2560]{2,1,0:T(2,128)(2,1)} %reshape.390), calls=%async_computation.1 | async-start | bytes 655360 | tf_op jit(solution)/shard_map/while/body/eval_jaxpr/all_to_all | solution.py:102
  130.3 4.5 copy-start.2
  139.3 13.4 %all-to-all-start = ((bf16[32,2,2560]{2,1,0:T(2,128)(2,1)}), bf16[32,2,2560]{2,1,0:T(2,128)(2,1)S(1)}, u32[]{:S(2)}, u32[]{:S(2)}) async-start(bf16[32,2,2560]{2,1,0:T(2,128)(2,1)} %reshape.387), calls=%async_computation | async-start | bytes 655360 | tf_op jit(solution)/shard_map/while/body/eval_jaxpr/all_to_all | solution.py:98
  174.8 13.4 %all-to-all-start.1 = ((bf16[32,2,2560]{2,1,0:T(2,128)(2,1)}), bf16[32,2,2560]{2,1,0:T(2,128)(2,1)S(1)}, u32[]{:S(2)}, u32[]{:S(2)}) async-start(bf16[32,2,2560]{2,1,0:T(2,128)(2,1)} %reshape.390), calls=%async_computation.1 | async-start | bytes 655360 | tf_op jit(solution)/shard_map/while/body/eval_jaxpr/all_to_all | solution.py:102
  193.9 4.5 copy-start.2
  202.9 13.4 %all-to-all-start = ((bf16[32,2,2560]{2,1,0:T(2,128)(2,1)}), bf16[32,2,2560]{2,1,0:T(2,128)(2,1)S(1)}, u32[]{:S(2)}, u32[]{:S(2)}) async-start(bf16[32,2,2560]{2,1,0:T(2,128)(2,1)} %reshape.387), calls=%async_computation | async-start | bytes 655360 | tf_op jit(solution)/shard_map/while/body/eval_jaxpr/all_to_all | solution.py:98
  238.5 13.4 %all-to-all-start.1 = ((bf16[32,2,2560]{2,1,0:T(2,128)(2,1)}), bf16[32,2,2560]{2,1,0:T(2,128)(2,1)S(1)}, u32[]{:S(2)}, u32[]{:S(2)}) async-start(bf16[32,2,2560]{2,1,0:T(2,128)(2,1)} %reshape.390), calls=%async_computation.1 | async-start | bytes 655360 | tf_op jit(solution)/shard_map/while/body/eval_jaxpr/all_to_all | solution.py:102
  257.6 4.5 copy-start.2
  266.6 13.4 %all-to-all-start = ((bf16[32,2,2560]{2,1,0:T(2,128)(2,1)}), bf16[32,2,2560]{2,1,0:T(2,128)(2,1)S(1)}, u32[]{:S(2)}, u32[]{:S(2)}) async-start(bf16[32,2,2560]{2,1,0:T(2,128)(2,1)} %reshape.387), calls=%async_computation | async-start | bytes 655360 | tf_op jit(solution)/shard_map/while/body/eval_jaxpr/all_to_all | solution.py:98
  302.1 13.4 %all-to-all-start.1 = ((bf16[32,2,2560]{2,1,0:T(2,128)(2,1)}), bf16[32,2,2560]{2,1,0:T(2,128)(2,1)S(1)}, u32[]{:S(2)}, u32[]{:S(2)}) async-start(bf16[32,2,2560]{2,1,0:T(2,128)(2,1)} %reshape.390), calls=%async_computation.1 | async-start | bytes 655360 | tf_op jit(solution)/shard_map/while/body/eval_jaxpr/all_to_all | solution.py:102
  321.2 4.5 copy-start.2
  330.2 13.4 %all-to-all-start = ((bf16[32,2,2560]{2,1,0:T(2,128)(2,1)}), bf16[32,2,2560]{2,1,0:T(2,128)(2,1)S(1)}, u32[]{:S(2)}, u32[]{:S(2)}) async-start(bf16[32,2,2560]{2,1,0:T(2,128)(2,1)} %reshape.387), calls=%async_computation | async-start | bytes 655360 | tf_op jit(solution)/shard_map/while/body/eval_jaxpr/all_to_all | solution.py:98
  365.8 13.4 %all-to-all-start.1 = ((bf16[32,2,2560]{2,1,0:T(2,128)(2,1)}), bf16[32,2,2560]{2,1,0:T(2,128)(2,1)S(1)}, u32[]{:S(2)}, u32[]{:S(2)}) async-start(bf16[32,2,2560]{2,1,0:T(2,128)(2,1)} %reshape.390), calls=%async_computation.1 | async-start | bytes 655360 | tf_op jit(solution)/shard_map/while/body/eval_jaxpr/all_to_all | solution.py:102
  384.9 4.5 copy-start.2
  393.9 13.4 %all-to-all-start = ((bf16[32,2,2560]{2,1,0:T(2,128)(2,1)}), bf16[32,2,2560]{2,1,0:T(2,128)(2,1)S(1)}, u32[]{:S(2)}, u32[]{:S(2)}) async-start(bf16[32,2,2560]{2,1,0:T(2,128)(2,1)} %reshape.387), calls=%async_computation | async-start | bytes 655360 | tf_op jit(solution)/shard_map/while/body/eval_jaxpr/all_to_all | solution.py:98
  429.4 13.4 %all-to-all-start.1 = ((bf16[32,2,2560]{2,1,0:T(2,128)(2,1)}), bf16[32,2,2560]{2,1,0:T(2,128)(2,1)S(1)}, u32[]{:S(2)}, u32[]{:S(2)}) async-start(bf16[32,2,2560]{2,1,0:T(2,128)(2,1)} %reshape.390), calls=%async_computation.1 | async-start | bytes 655360 | tf_op jit(solution)/shard_map/while/body/eval_jaxpr/all_to_all | solution.py:102
  448.5 4.5 copy-start.2
  457.5 13.4 %all-to-all-start = ((bf16[32,2,2560]{2,1,0:T(2,128)(2,1)}), bf16[32,2,2560]{2,1,0:T(2,128)(2,1)S(1)}, u32[]{:S(2)}, u32[]{:S(2)}) async-start(bf16[32,2,2560]{2,1,0:T(2,128)(2,1)} %reshape.387), calls=%async_computation | async-start | bytes 655360 | tf_op jit(solution)/shard_map/while/body/eval_jaxpr/all_to_all | solution.py:98
  493.0 13.4 %all-to-all-start.1 = ((bf16[32,2,2560]{2,1,0:T(2,128)(2,1)}), bf16[32,2,2560]{2,1,0:T(2,128)(2,1)S(1)}, u32[]{:S(2)}, u32[]{:S(2)}) async-start(bf16[32,2,2560]{2,1,0:T(2,128)(2,1)} %reshape.390), calls=%async_computation.1 | async-start | bytes 655360 | tf_op jit(solution)/shard_map/while/body/eval_jaxpr/all_to_all | solution.py:102
  512.1 4.5 copy-start.2
  521.2 13.4 %all-to-all-start = ((bf16[32,2,2560]{2,1,0:T(2,128)(2,1)}), bf16[32,2,2560]{2,1,0:T(2,128)(2,1)S(1)}, u32[]{:S(2)}, u32[]{:S(2)}) async-start(bf16[32,2,2560]{2,1,0:T(2,128)(2,1)} %reshape.387), calls=%async_computation | async-start | bytes 655360 | tf_op jit(solution)/shard_map/while/body/eval_jaxpr/all_to_all | solution.py:98
  556.7 13.4 %all-to-all-start.1 = ((bf16[32,2,2560]{2,1,0:T(2,128)(2,1)}), bf16[32,2,2560]{2,1,0:T(2,128)(2,1)S(1)}, u32[]{:S(2)}, u32[]{:S(2)}) async-start(bf16[32,2,2560]{2,1,0:T(2,128)(2,1)} %reshape.390), calls=%async_computation.1 | async-start | bytes 655360 | tf_op jit(solution)/shard_map/while/body/eval_jaxpr/all_to_all | solution.py:102
  575.8 4.5 copy-start.2
  584.8 13.4 %all-to-all-start = ((bf16[32,2,2560]{2,1,0:T(2,128)(2,1)}), bf16[32,2,2560]{2,1,0:T(2,128)(2,1)S(1)}, u32[]{:S(2)}, u32[]{:S(2)}) async-start(bf16[32,2,2560]{2,1,0:T(2,128)(2,1)} %reshape.387), calls=%async_computation | async-start | bytes 655360 | tf_op jit(solution)/shard_map/while/body/eval_jaxpr/all_to_all | solution.py:98
  620.3 13.4 %all-to-all-start.1 = ((bf16[32,2,2560]{2,1,0:T(2,128)(2,1)}), bf16[32,2,2560]{2,1,0:T(2,128)(2,1)S(1)}, u32[]{:S(2)}, u32[]{:S(2)}) async-start(bf16[32,2,2560]{2,1,0:T(2,128)(2,1)} %reshape.390), calls=%async_computation.1 | async-start | bytes 655360 | tf_op jit(solution)/shard_map/while/body/eval_jaxpr/all_to_all | solution.py:102
  639.4 4.4 copy-start.2
  648.4 13.4 %all-to-all-start = ((bf16[32,2,2560]{2,1,0:T(2,128)(2,1)}), bf16[32,2,2560]{2,1,0:T(2,128)(2,1)S(1)}, u32[]{:S(2)}, u32[]{:S(2)}) async-start(bf16[32,2,2560]{2,1,0:T(2,128)(2,1)} %reshape.387), calls=%async_computation | async-start | bytes 655360 | tf_op jit(solution)/shard_map/while/body/eval_jaxpr/all_to_all | solution.py:98
  684.0 13.4 %all-to-all-start.1 = ((bf16[32,2,2560]{2,1,0:T(2,128)(2,1)}), bf16[32,2,2560]{2,1,0:T(2,128)(2,1)S(1)}, u32[]{:S(2)}, u32[]{:S(2)}) async-start(bf16[32,2,2560]{2,1,0:T(2,128)(2,1)} %reshape.390), calls=%async_computation.1 | async-start | bytes 655360 | tf_op jit(solution)/shard_map/while/body/eval_jaxpr/all_to_all | solution.py:102
  703.1 4.5 copy-start.2
  712.1 13.4 %all-to-all-start = ((bf16[32,2,2560]{2,1,0:T(2,128)(2,1)}), bf16[32,2,2560]{2,1,0:T(2,128)(2,1)S(1)}, u32[]{:S(2)}, u32[]{:S(2)}) async-start(bf16[32,2,2560]{2,1,0:T(2,128)(2,1)} %reshape.387), calls=%async_computation | async-start | bytes 655360 | tf_op jit(solution)/shard_map/while/body/eval_jaxpr/all_to_all | solution.py:98
  747.6 13.4 %all-to-all-start.1 = ((bf16[32,2,2560]{2,1,0:T(2,128)(2,1)}), bf16[32,2,2560]{2,1,0:T(2,128)(2,1)S(1)}, u32[]{:S(2)}, u32[]{:S(2)}) async-start(bf16[32,2,2560]{2,1,0:T(2,128)(2,1)} %reshape.390), calls=%async_computation.1 | async-start | bytes 655360 | tf_op jit(solution)/shard_map/while/body/eval_jaxpr/all_to_all | solution.py:102
  766.7 4.5 copy-start.2
  771.4 10.2 %copy-start.10 = (s32[2,40]{1,0:T(2,128)S(1)}, s32[2,40]{1,0:T(2,128)}, u32[]{:S(2)}) copy-start(s32[2,40]{1,0:T(2,128)} %param.34) | copy-start | bytes 964
  772.2 12.2 %collective-permute-start = (bf16[12,1,8,256]{3,2,0,1:T(8,128)(2,1)S(1)}, bf16[12,1,8,256]{3,2,0,1:T(8,128)(2,1)S(1)}, u32[]{:S(2)}, u32[]{:S(2)}) collective-permute-start(bf16[12,1,8,256]{3,2,0,1:T(8,128)(2,1)S(1)} %get-tuple-element.343), channel_id=1, source_target_pairs={{0,4},{4,8},{8,12},{12,16},{16,20},{20,24},{24,28},{28,32},{32,36}... | collective-permute-start | bytes 147464 | tf_op jit(solution)/shard_map/ppermute | solution.py:22
  775.4 9.0 collective-permute-start.1
  947.7 48.8 %copy-start.3 = (f32[1,32,1440]{2,1,0:T(8,128)}, f32[1,32,1440]{2,1,0:T(8,128)S(1)}, u32[]{:S(2)}) copy-start(f32[1,32,1440]{2,1,0:T(8,128)S(1)} %get-tuple-element.267) | copy-start | bytes 552964
  947.7 40.6 %copy-start.16 = (f32[40]{0:T(128)S(1)}, f32[40]{0:T(128)}, u32[]{:S(2)}) copy-start(f32[40]{0:T(128)} %param.35) | copy-start | bytes 484
  948.2 40.7 %collective-permute-start.2 = (bf16[12,1,32,256]{3,2,0,1:T(8,128)(2,1)S(1)}, bf16[12,1,32,256]{3,2,0,1:T(8,128)(2,1)S(1)}, u32[]{:S(2)}, u32[]{:S(2)}) collective-permute-start(bf16[12,1,32,256]{3,2,0,1:T(8,128)(2,1)S(1)} %fusion.46), channel_id=1, source_target_pairs={{0,4},{4,8},{8,12},{12,16},{16,20},{20,24},{24,28},{28,32},{32,36}... | collective-permute-start | bytes 589832 | tf_op jit(solution)/shard_map/ppermute | solution.py:22
  986.3 9.1 collective-permute-start.3
  (19 other events, 21.0 us)
